TPU v7x, 256 devices: a whole 4x4x8 slice. The times are simulated.
256 devices in a mesh: dp: 16 (over x_lo, z), shard: 16 (over x_hi, y, core).
Axes of the slice: x: 4 (x_hi: 2, x_lo: 2; x = x_hi * 2 + x_lo), y: 4, z: 8, core: 2. Of those that a mesh axis runs over, the one named last changes fastest.
Arguments:
- gradient: bfloat16 [16, 2560, 2560], P(None, ('shard', 'dp')), may hold values from -1.5 to 1.5
- owner: int32 [16], replicated, may hold values from 0 to 15, each once
- a_inverse: bfloat16 [16, 2560, 2560], P('dp', 'shard'), as said below
- b_inverse: bfloat16 [16, 2560, 2560], P('dp', 'shard'), as said below
Outputs:
- preconditioned: bfloat16 [16, 2560, 2560], P(None, ('shard', 'dp'))
Inputs may be any that keep to these rules, and one draw needn't show every extreme that they name: owner names each of the 16 slots for exactly one layer. Every slot of a_inverse is a symmetric matrix. Every slot of b_inverse is a symmetric matrix.
All inputs are finite; a program needn't handle non-finite values.
Results may differ from a plain program's by a relative error of at most 0.0049.
Values may be sent and summed in bfloat16 or wider, within the bound.
No kernel may reach another device: no remote copies, remote signals or barrier semaphores. Data moves between devices by JAX's collectives and lax.ppermute only.
A program may use at most 128 MiB of HBM per device.

v0:
```python
import jax
import jax.numpy as jnp
from jax import lax
from jax.sharding import PartitionSpec as P


def local(gradient, owner, a_inverse, b_inverse):
    layer_count = gradient.shape[0]
    chosen = (owner[:, None] == jnp.arange(layer_count, dtype=jnp.int32)[None, :]).astype(
        jnp.bfloat16
    )
    outgoing = jnp.einsum(
        "lo,lrc->orc", chosen, gradient, preferred_element_type=jnp.float32
    ).astype(jnp.bfloat16)
    owned = lax.all_to_all(outgoing, "dp", split_axis=0, concat_axis=1, tiled=True)
    grad_rows = owned[0]
    right_rows = b_inverse[0]
    left_rows = a_inverse[0]
    columns = grad_rows
    right_half = jnp.dot(
        columns,
        lax.all_gather(right_rows, "shard", axis=0, tiled=True),
        preferred_element_type=jnp.float32,
    ).astype(jnp.bfloat16)
    columns = left_rows
    summed = jnp.dot(
        columns,
        lax.all_gather(right_half, "shard", axis=0, tiled=True),
        preferred_element_type=jnp.float32,
    )
    result_rows = summed.astype(jnp.bfloat16)
    returned = lax.all_to_all(
        result_rows[None, :, :], "dp", split_axis=1, concat_axis=0, tiled=True
    )
    return jnp.take(returned, owner, axis=0)


def solution(mesh):
    in_specs = (P(None, ("shard", "dp"), None), P(), P("dp", "shard", None), P("dp", "shard", None))
    out_specs = P(None, ("shard", "dp"), None)
    return jax.shard_map(local, mesh=mesh, in_specs=in_specs, out_specs=out_specs, check_vma=False)
```

profile of v0, /device:TPU:32, one launch (start us, length us, event | category | flops | bytes accessed | tf_op | source)
XLA Modules:
  0.0 281.3 jit_solution(5845131515558374198)
XLA Ops:
  6.5 0.0 copy-start
  6.5 0.0 all-gather.6.cloned.1.call-start
  6.5 0.7 all-gather.6.cloned.1.call-update
  7.3 0.0 all-gather.4.cloned.1.call-start
  7.3 0.4 copy-done
  7.7 1.0 convolution_convert_fusion.1
  8.7 0.5 copy.7
  9.2 42.1 %all_to_all.21 = bf16[16,10,2560]{2,1,0:T(8,128)(2,1)S(1)} all-to-all(bf16[16,10,2560]{2,1,0:T(8,128)(2,1)S(1)} %copy.7), channel_id=1, replica_groups=mesh['dp'=16,'shard'=16] {'dp'}, dimensions={0} | all-to-all | bytes 1638400 | tf_op jit(solution)/shard_map/all_to_all | solution.py:15
  51.3 0.3 squeeze.9
  51.6 0.0 copy-start.2
  51.6 66.0 %all-gather.6.cloned.1.call-done = bf16[1,2560,2560]{2,1,0:T(8,128)(2,1)} async-done(((bf16[1,160,2560]{2,1,0:T(8,128)(2,1)}), bf16[1,2560,2560]{2,1,0:T(8,128)(2,1)}) %all-gather.6.cloned.1.call-update) | async-done | bytes 13107216 | tf_op jit(solution)/shard_map/all_gather | solution.py:22
  117.6 7.9 %fusion.2 = bf16[160,2560]{1,0:T(8,128)(2,1)} fusion(bf16[160,2560]{1,0:T(8,128)(2,1)S(1)} %squeeze.9, bf16[1,2560,2560]{2,1,0:T(8,128)(2,1)} %all-gather.6.cloned.1.call-done), kind=kOutput, calls=%fused_computation.3 | convolution fusion | flops 2097561600 | bytes 14745600 | tf_op jit(solution)/shard_map/dot_general | solution.py:20
  125.5 0.0 all-gather.4.cloned.1.call-update
  125.5 95.9 %all-gather.4.cloned.1.call-done = bf16[2560,2560]{1,0:T(8,128)(2,1)} async-done(((bf16[160,2560]{1,0:T(8,128)(2,1)}), bf16[2560,2560]{1,0:T(8,128)(2,1)}) %all-gather.4.cloned.1.call-update) | async-done | bytes 13107216 | tf_op jit(solution)/shard_map/all_gather | solution.py:28
  221.5 0.0 copy-done.2
  221.5 7.0 %fusion.5 = bf16[1,160,2560]{2,1,0:T(8,128)(2,1)S(1)} fusion(bf16[2560,2560]{1,0:T(8,128)(2,1)} %all-gather.4.cloned.1.call-done, bf16[1,160,2560]{2,1,0:T(8,128)(2,1)S(1)} %copy-done.2), kind=kOutput, calls=%fused_computation.6 | convolution fusion | flops 2097561600 | bytes 14745600 | tf_op jit(solution)/shard_map/dot_general | solution.py:26
  228.5 1.3 copy.12
  229.8 0.5 broadcast.17
  230.3 5.6 %reduce.2 = bf16[160,2560]{1,0:T(8,128)(2,1)S(1)} reduce(bf16[160,1,2560]{2,1,0:T(2,128)(2,1)S(1)} %bitcast.23, bf16[]{:T(256)} %broadcast.17), dimensions={1}, to_apply=%bitcast.22.reduce_sub_computation | reduce | bytes 1638402
  235.9 0.0 copy-start.1
  235.9 1.3 reshape.25
  237.2 7.5 %all-to-all-start.1 = ((bf16[16,2,12800]{2,1,0:T(2,128)(2,1)}), bf16[16,2,12800]{2,1,0:T(2,128)(2,1)S(1)}, u32[]{:S(2)}, u32[]{:S(2)}) async-start(bf16[16,2,12800]{2,1,0:T(2,128)(2,1)} %reshape.25), calls=%async_computation.1 | async-start | bytes 1638400 | tf_op jit(solution)/shard_map/all_to_all | solution.py:32
  244.7 0.0 copy-done.1
  244.7 21.8 %all-to-all-done.1 = bf16[16,2,12800]{2,1,0:T(2,128)(2,1)S(1)} async-done(((bf16[16,2,12800]{2,1,0:T(2,128)(2,1)}), bf16[16,2,12800]{2,1,0:T(2,128)(2,1)S(1)}, u32[]{:S(2)}, u32[]{:S(2)}) %all-to-all-start.1) | async-done | bytes 819232 | tf_op jit(solution)/shard_map/all_to_all | solution.py:32
  266.6 0.7 reshape.26
  267.2 4.7 %bitcast_reduce_fusion = bf16[160,2560]{1,0:T(8,128)(2,1)S(1)} fusion(bf16[160,1,2560]{2,1,0:T(2,128)(2,1)S(1)} %reshape.26), kind=kLoop, calls=%fused_computation.15 | loop fusion | bytes 1638400 | tf_op jit(solution)/shard_map/all_to_all | solution.py:32
  271.9 0.3 all_to_all.8
  272.3 0.6 gather_fusion
  272.9 0.2 broadcast_select_fusion
  273.1 1.3 copy.9
  (3 shorter events, 0.0 us)
Async XLA Ops:
  6.5 1.1 copy-start
  6.5 111.1 %all-gather.6.cloned.1.call-start = ((), (), s32[]{:S(2)}) async-start(), calls=%async_computation.3 | async-start | bytes 13926400 | tf_op jit(solution)/shard_map/all_gather | solution.py:22
  7.3 214.2 %all-gather.4.cloned.1.call-start = ((), (), s32[]{:S(2)}) async-start(), calls=%async_computation.2 | async-start | bytes 13926400 | tf_op jit(solution)/shard_map/all_gather | solution.py:28
  51.6 169.9 %copy-start.2 = (bf16[1,160,2560]{2,1,0:T(8,128)(2,1)S(1)}, bf16[1,160,2560]{2,1,0:T(8,128)(2,1)}, u32[]{:S(2)}) copy-start(bf16[1,160,2560]{2,1,0:T(8,128)(2,1)} %param.6) | copy-start | bytes 2457604
  235.9 8.8 %copy-start.1 = (s32[16]{0:T(128)S(1)}, s32[16]{0:T(128)}, u32[]{:S(2)}) copy-start(s32[16]{0:T(128)} %param.5) | copy-start | bytes 196
  237.2 29.4 %all-to-all-start.1 = ((bf16[16,2,12800]{2,1,0:T(2,128)(2,1)}), bf16[16,2,12800]{2,1,0:T(2,128)(2,1)S(1)}, u32[]{:S(2)}, u32[]{:S(2)}) async-start(bf16[16,2,12800]{2,1,0:T(2,128)(2,1)} %reshape.25), calls=%async_computation.1 | async-start | bytes 1638400 | tf_op jit(solution)/shard_map/all_to_all | solution.py:32
Sparse Core Ops, SparseCore 0:
  10.1 107.4 all-gather.5
  125.7 95.7 all-gather.3
where the time goes:
time: 282 us; the launch traced here: 281 us
  waiting for transfers between devices  185 us (66%)
  blocking collectives  42.1 us (15%)
  matrix products  15.9 us (6%)
  between operations  13.5 us (5%)
  local copies, waits for them, and re-layouts  11.9 us (4%)
  starting transfers between devices  7.54 us (3%)
  other arithmetic  5.81 us (2%)
    all_gather x1, waiting for transfers between devices, local(): lax.all_gather(right_half, 'shard', axis=0, tiled=True)  95.9 us
    all_gather x1, waiting for transfers between devices, local(): lax.all_gather(right_rows, 'shard', axis=0, tiled=True)  66 us
    all_to_all x1, blocking collectives, local(): lax.all_to_all(outgoing, 'dp', split_axis=0, concat_axis=1, tiled=True)  42.1 us
    all_to_all x1, waiting for transfers between devices, local(): lax.all_to_all(result_rows[None, :, :], 'dp', split_axis=1, concat_axis=0...  21.8 us
    dot_general x1, matrix products, local(): jnp.dot(columns, lax.all_gather(right_rows, 'shard', axis=0, tiled=True),...  7.9 us
    all_to_all x1, starting transfers between devices, local(): lax.all_to_all(result_rows[None, :, :], 'dp', split_axis=1, concat_axis=0...  7.5 us
    dot_general x1, matrix products, local(): jnp.dot(columns, lax.all_gather(right_half, 'shard', axis=0, tiled=True),...  7 us
  transfers between devices with their start and end apart: 3, of which 3 were waited for; matrix products, arithmetic and copies ran while one was open for 1% of the time, Pallas kernels for 0%

commit v1 on v0

v1 whole, which is shorter than its diff:
```python
import jax
import jax.numpy as jnp
from jax import lax
from jax.experimental import pallas as pl
from jax.experimental.pallas import tpu as pltpu
from jax.sharding import Mesh, PartitionSpec as P

AXES = ("xl", "z", "xh", "y", "c")
SIZES = dict(xl=2, z=8, xh=2, y=4, c=2)
DP = ("xl", "z")
ROWS = 10
SLOTS = 16
BLOCK = ROWS * SLOTS
PARTS = 4
VMEM_LIMIT = 48 * 1024 * 1024
F32 = jnp.float32
BF16 = jnp.bfloat16


def shift(value, axis, by):
    n = SIZES[axis]
    return lax.ppermute(value, axis, [(i, (i + by) % n) for i in range(n)])


def params():
    return pltpu.CompilerParams(vmem_limit_bytes=VMEM_LIMIT)


def onehot(hit):
    return jnp.where(hit, 1.0, 0.0).astype(BF16)


def vspec():
    return pl.BlockSpec(memory_space=pltpu.VMEM)


def aspec():
    return pl.BlockSpec(memory_space=pl.ANY)


def sspec():
    return pl.BlockSpec(memory_space=pltpu.SMEM)


def pack_kernel(base_ref, part_ref, *refs):
    x_refs, o_ref = refs[:-1], refs[-1]
    rows = PARTS * BLOCK
    width = o_ref.shape[1]
    row = lax.broadcasted_iota(jnp.int32, (rows, BLOCK), 0)
    total = None
    for q in range(PARTS):
        pick = onehot(row == base_ref[...] + ROWS * part_ref[q])
        x = x_refs[q][...] if len(x_refs) > 1 else x_refs[0][:, q * width : (q + 1) * width]
        term = jnp.dot(pick, x, preferred_element_type=F32)
        total = term if total is None else total + term
    o_ref[...] = total.astype(BF16)


def pack(base, parts, xs):
    width = 640
    return pl.pallas_call(
        pack_kernel,
        out_shape=jax.ShapeDtypeStruct((PARTS * BLOCK, width), BF16),
        in_specs=[vspec(), sspec()] + [vspec()] * len(xs),
        out_specs=vspec(),
        compiler_params=params(),
        name="pack",
    )(base, parts, *xs)


def unpack_kernel(interleave, base_ref, x_ref, o_ref):
    width = x_ref.shape[1]
    col = lax.broadcasted_iota(jnp.int32, (BLOCK, PARTS * BLOCK), 1)
    for q in range(PARTS):
        pick = onehot(col == base_ref[...] + ROWS * q)
        block = jnp.dot(pick, x_ref[...], preferred_element_type=F32)
        if not interleave:
            o_ref[:, q * width : (q + 1) * width] = block.astype(BF16)
            continue
        xh, c = q // 2, q % 2
        for y in range(4):
            at = (xh * 8 + y * 2 + c) * BLOCK
            o_ref[:, at : at + BLOCK] = block[:, y * BLOCK : (y + 1) * BLOCK].astype(BF16)


def unpack(base, x, interleave):
    import functools

    return pl.pallas_call(
        functools.partial(unpack_kernel, interleave),
        out_shape=jax.ShapeDtypeStruct((BLOCK, PARTS * x.shape[1]), BF16),
        in_specs=[vspec(), vspec()],
        out_specs=vspec(),
        compiler_params=params(),
        name="unpack",
    )(base, x)


def right_kernel(count, at_ref, *refs):
    g_refs, b_refs = refs[:count], refs[count : count + 4]
    o_refs, (b_all, sem) = refs[count + 4 : 2 * count + 4], refs[2 * count + 4 :]
    copies = [
        pltpu.make_async_copy(b, b_all.at[pl.ds(pl.multiple_of(at_ref[n], 32), BLOCK)], sem.at[n])
        for n, b in enumerate(b_refs)
    ]
    for copy in copies:
        copy.start()
    for copy in copies:
        copy.wait()
    for g, o in zip(g_refs, o_refs):
        o[...] = lax.dot_general(
            g[...], b_all[...], (((1,), (1,)), ((), ())), preferred_element_type=F32
        ).astype(BF16)


def right(at, gs, bs):
    import functools

    n = len(gs)
    return pl.pallas_call(
        functools.partial(right_kernel, n),
        out_shape=[jax.ShapeDtypeStruct((BLOCK, 4 * BLOCK), BF16)] * n,
        in_specs=[sspec()] + [vspec()] * n + [aspec()] * 4,
        out_specs=[vspec()] * n,
        scratch_shapes=[pltpu.VMEM((4 * BLOCK, gs[0].shape[1]), BF16), pltpu.SemaphoreType.DMA((4,))],
        compiler_params=params(),
        cost_estimate=pl.CostEstimate(
            flops=2 * n * BLOCK * 640 * 2560, bytes_accessed=(n + 4) * BLOCK * 2560 * 2, transcendentals=0
        ),
        name="right",
    )(at, *gs, *bs)


def left_kernel(count, at_ref, *refs):
    a_refs, r_refs = refs[:count], refs[count : count + 16]
    o_refs, (r_all, sem) = refs[count + 16 : 2 * count + 16], refs[2 * count + 16 :]
    copies = [
        pltpu.make_async_copy(r, r_all.at[pl.ds(pl.multiple_of(at_ref[n], 32), BLOCK)], sem.at[n])
        for n, r in enumerate(r_refs)
    ]
    for copy in copies:
        copy.start()
    for copy in copies:
        copy.wait()
    for a, o in zip(a_refs, o_refs):
        o[...] = jnp.dot(a[...], r_all[...], preferred_element_type=F32).astype(BF16)


def left(at, blocks, rs):
    import functools

    n = len(blocks)
    return pl.pallas_call(
        functools.partial(left_kernel, n),
        out_shape=[jax.ShapeDtypeStruct((BLOCK, 4 * BLOCK), BF16)] * n,
        in_specs=[sspec()] + [vspec()] * n + [aspec()] * 16,
        out_specs=[vspec()] * n,
        scratch_shapes=[pltpu.VMEM((16 * BLOCK, 4 * BLOCK), BF16), pltpu.SemaphoreType.DMA((16,))],
        compiler_params=params(),
        cost_estimate=pl.CostEstimate(
            flops=2 * n * BLOCK * 640 * 2560, bytes_accessed=(n + 4) * BLOCK * 2560 * 2, transcendentals=0
        ),
        name="left",
    )(at, *blocks, *rs)


def around(value):
    over_x = shift(value, "xh", 1)
    return [value, shift(value, "c", 1), over_x, shift(over_x, "c", 1)]


def along(value):
    return [value, shift(value, "y", 1), shift(value, "y", -1), shift(value, "y", 2)]


def exchange(x):
    width = x.shape[1]
    x = x.reshape(SLOTS, PARTS * ROWS, width)
    return lax.all_to_all(x, DP, split_axis=0, concat_axis=0, tiled=True).reshape(-1, width)


def local(gradient, owner, a_inverse, b_inverse):
    xh, y, c = (lax.axis_index(n) for n in ("xh", "y", "c"))
    a, b = a_inverse[0], b_inverse[0]
    features = gradient.shape[2]
    m = jnp.arange(BLOCK, dtype=jnp.int32)
    natural = (m // ROWS) * (PARTS * ROWS) + m % ROWS
    by_layer = jnp.tile(owner, ROWS) * (PARTS * ROWS) + m // SLOTS
    in_order = jnp.arange(PARTS, dtype=jnp.int32)
    near = [(xh, c), (xh, 1 - c), (1 - xh, c), (1 - xh, 1 - c)]
    ys = [y, (y + 3) % 4, (y + 1) % 4, (y + 2) % 4]

    rows = gradient.transpose(1, 0, 2).reshape(BLOCK, features)
    bs = along(b)
    g = unpack(natural[:, None], exchange(pack(by_layer[None, :], in_order, [rows])), False)
    blocks = around(a)
    r = right(jnp.stack(ys).astype(jnp.int32) * BLOCK, around(g), bs)
    moved = [along(v) for v in r]
    at = jnp.stack([(u * 8 + v * 2 + w) * BLOCK for u, w in near for v in ys]).astype(jnp.int32)
    out = left(at, blocks, [moved[n][k] for n in range(4) for k in range(4)])
    swap = lambda v: lax.ppermute(v, ("xh", "c"), [(i, 3 - i) for i in range(4)])
    mine = [out[0], shift(out[1], "c", 1), shift(out[2], "xh", 1), swap(out[3])]
    parts = jnp.stack([u * 2 + w for u, w in near]).astype(jnp.int32)
    done = unpack(by_layer[:, None], exchange(pack(natural[None, :], parts, mine)), True)
    return done.reshape(ROWS, SLOTS, features).transpose(1, 0, 2)


def solution(mesh):
    fine = Mesh(mesh.devices.reshape(tuple(SIZES[n] for n in AXES)), AXES)
    rows = ("xh", "y", "c")
    in_specs = (P(None, rows + DP, None), P(), P(DP, rows, None), P(DP, rows, None))
    return jax.shard_map(
        local, mesh=fine, in_specs=in_specs, out_specs=P(None, rows + DP, None), check_vma=False
    )
```

time: 282 us -> 185 us (0.66)
  waiting for transfers between devices: 185 us -> 104 us
  blocking collectives: 42.1 us -> 0 us
  starting transfers between devices: 7.54 us -> 48.5 us
  Pallas kernels: 0 us -> 24.3 us
  matrix products: 15.9 us -> 0 us
  between operations: 13.5 us -> 0.13 us
  local copies, waits for them, and re-layouts: 11.9 us -> 5.94 us
  other arithmetic: 5.81 us -> 0.89 us
    all_gather x2 -> x0, waiting for transfers between devices: 162 us -> none  [the longest x1 95.9 us: local(): lax.all_gather(right_half, 'shard', axis=0, tiled=True)]
    ppermute x0 -> x24, waiting for transfers between devices: none -> 62.9 us  [the longest x23 59.5 us: shift(): return lax.ppermute(value, axis, [(i, (i + by) % n) for i in range(n)])]
    all_to_all x1 -> x0, blocking collectives: 42.1 us -> none  [local(): lax.all_to_all(outgoing, 'dp', split_axis=0, concat_axis=1, tiled=True)]
    ppermute x0 -> x24, starting transfers between devices: none -> 31.8 us  [the longest x23 29.3 us: shift(): return lax.ppermute(value, axis, [(i, (i + by) % n) for i in range(n)])]
    pallas_call x0 -> x6, Pallas kernels: none -> 24.3 us  [the longest x1 8.29 us: right(): pl.pallas_call(functools.partial(right_kernel, n), out_shape=[jax.ShapeDt...]
    all_to_all x1 -> x2, waiting for transfers between devices: 21.8 us -> 41.6 us  [exchange(): lax.all_to_all(x, DP, split_axis=0, concat_axis=0, tiled=True)]
    dot_general x3 -> x0, matrix products: 15.9 us -> none  [the longest x1 7.9 us: local(): jnp.dot(columns, lax.all_gather(right_rows, 'shard', axis=0, tiled=True),...]
    all_to_all x1 -> x2, starting transfers between devices: 7.5 us -> 16.7 us  [exchange(): lax.all_to_all(x, DP, split_axis=0, concat_axis=0, tiled=True)]
  transfers between devices with their start and end apart: 3 -> 26, of which waited for: 3 -> 14; matrix products, arithmetic and copies ran while one was open for 1% -> 0% of each run, Pallas kernels for 0% -> 5%
where the time goes in v1:
time: 185 us; the launch traced here: 184 us
  waiting for transfers between devices  104 us (56%)
  starting transfers between devices  48.5 us (26%)
  Pallas kernels  24.3 us (13%)
  local copies, waits for them, and re-layouts  5.94 us (3%)
    ppermute x23, waiting for transfers between devices, shift(): return lax.ppermute(value, axis, [(i, (i + by) % n) for i in range(n)])  59.5 us
    all_to_all x2, waiting for transfers between devices, exchange(): lax.all_to_all(x, DP, split_axis=0, concat_axis=0, tiled=True)  41.6 us
    ppermute x23, starting transfers between devices, shift(): return lax.ppermute(value, axis, [(i, (i + by) % n) for i in range(n)])  29.3 us
    all_to_all x2, starting transfers between devices, exchange(): lax.all_to_all(x, DP, split_axis=0, concat_axis=0, tiled=True)  16.7 us
    pallas_call x1, Pallas kernels, right(): pl.pallas_call(functools.partial(right_kernel, n), out_shape=[jax.ShapeDt...  8.29 us
    pallas_call x1, Pallas kernels, left(): pl.pallas_call(functools.partial(left_kernel, n), out_shape=[jax.ShapeDty...  7.91 us
    unnamed x16, local copies, waits for them, and re-layouts  5.67 us
    pallas_call x2, Pallas kernels, pack(): pl.pallas_call(pack_kernel, out_shape=jax.ShapeDtypeStruct((PARTS * BLOCK...  5.25 us
  transfers between devices with their start and end apart: 26, of which 14 were waited for; matrix products, arithmetic and copies ran while one was open for 0% of the time, Pallas kernels for 5%

profile of v1, /device:TPU:32, one launch (start us, length us, event | category | flops | bytes accessed | tf_op | source)
XLA Modules:
  0.0 184.3 jit_solution(17621861398991554088)
XLA Ops:
  0.8 1.1 copy-done
  1.9 2.6 %pack.2 = bf16[640,640]{1,0:T(8,128)(2,1)} custom-call(s32[1,160]{1,0:T(1,128)S(1)} %fusion.12.base_ref, s32[4]{0:T(128)S(1)} %iota.24.part_ref, bf16[160,2560]{1,0:T(8,128)(2,1)S(1)} %bitcast.38), custom_call_target="tpu_custom_call" | custom-call | tf_op jit(solution)/shard_map/pack/pallas_call | solution.py:61
  4.5 9.6 %all-to-all-start = ((bf16[16,40,640]{2,1,0:T(8,128)(2,1)}), bf16[16,40,640]{2,1,0:T(8,128)(2,1)S(1)}, u32[]{:S(2)}, u32[]{:S(2)}) async-start(bf16[16,40,640]{2,1,0:T(8,128)(2,1)} %bitcast.27), calls=%async_computation | async-start | bytes 1638400 | tf_op jit(solution)/shard_map/all_to_all | solution.py:179
  14.2 1.7 collective-permute-start.6
  15.9 19.8 %all-to-all-done = bf16[16,40,640]{2,1,0:T(8,128)(2,1)S(1)} async-done(((bf16[16,40,640]{2,1,0:T(8,128)(2,1)}), bf16[16,40,640]{2,1,0:T(8,128)(2,1)S(1)}, u32[]{:S(2)}, u32[]{:S(2)}) %all-to-all-start) | async-done | bytes 819232 | tf_op jit(solution)/shard_map/all_to_all | solution.py:179
  36.6 2.8 %collective-permute-start.4 = (bf16[160,2560]{1,0:T(8,128)(2,1)S(1)}, bf16[160,2560]{1,0:T(8,128)(2,1)}, u32[]{:S(2)}, u32[]{:S(2)}) collective-permute-start(bf16[160,2560]{1,0:T(8,128)(2,1)S(1)} %unpack.2.refs_0_), channel_id=1, source_target_pairs={{0,8},{8,0},{1,9},{9,1},{2,10},{10,2},{3,11},{11,3},{4,12},{12,4},... | collective-permute-start | bytes 2457608 | tf_op jit(solution)/shard_map/ppermute | solution.py:22
  39.4 3.0 %collective-permute-start.7 = (bf16[160,2560]{1,0:T(8,128)(2,1)S(1)}, bf16[160,2560]{1,0:T(8,128)(2,1)S(1)}, u32[]{:S(2)}, u32[]{:S(2)}) collective-permute-start(bf16[160,2560]{1,0:T(8,128)(2,1)S(1)} %bitcast.40), channel_id=1, source_target_pairs={{0,6},{2,0},{4,2},{6,4},{1,7},{3,1},{5,3},{7,5},{8,14},{10,8},{12,... | collective-permute-start | bytes 2457608 | tf_op jit(solution)/shard_map/ppermute | solution.py:22
  43.9 15.6 %collective-permute-done.4.refs_2_ = bf16[160,2560]{1,0:T(8,128)(2,1)} collective-permute-done((bf16[160,2560]{1,0:T(8,128)(2,1)S(1)}, bf16[160,2560]{1,0:T(8,128)(2,1)}, u32[]{:S(2)}, u32[]{:S(2)}) %collective-permute-start.4) | collective-permute-done | bytes 819232 | tf_op jit(solution)/shard_map/ppermute | solution.py:22
  59.5 15.3 %collective-permute-done.7.refs_6_ = bf16[160,2560]{1,0:T(8,128)(2,1)S(1)} collective-permute-done((bf16[160,2560]{1,0:T(8,128)(2,1)S(1)}, bf16[160,2560]{1,0:T(8,128)(2,1)S(1)}, u32[]{:S(2)}, u32[]{:S(2)}) %collective-permute-start.7) | collective-permute-done | bytes 819232 | tf_op jit(solution)/shard_map/ppermute | solution.py:22
  75.8 8.3 %right.1 = (bf16[160,640]{1,0:T(8,128)(2,1)}, bf16[160,640]{1,0:T(8,128)(2,1)S(1)}, bf16[160,640]{1,0:T(8,128)(2,1)}, bf16[160,640]{1,0:T(8,128)(2,1)}) custom-call(s32[4]{0:T(128)S(1)} %add_multiply_fusion.at_ref, bf16[160,2560]{1,0:T(8,128)(2,1)S(1)} %unpack.2.refs_0_, bf16[160,2560]{1,0:T(8,128)(2,1)} %collective-permute-done.3.refs_1_, ...), custom_call_target="tpu_custom_call" | custom-call | flops 2097152000 | bytes 6553600 | tf_op jit(solution)/shard_map/right/pallas_call | solution.py:120
  84.1 3.8 %collective-permute-start.10 = (bf16[160,640]{1,0:T(8,128)(2,1)}, bf16[160,640]{1,0:T(8,128)(2,1)S(1)}, u32[]{:S(2)}, u32[]{:S(2)}) collective-permute-start(bf16[160,640]{1,0:T(8,128)(2,1)} %get-tuple-element.13.refs_4_), channel_id=1, source_target_pairs={{0,6},{2,0},{4,2},{6,4},{1,7},{3,1},{5,3},{7,5},{8,14},{10,8},{12,... | collective-permute-start | bytes 614408 | tf_op jit(solution)/shard_map/ppermute | solution.py:22
  89.7 2.3 %collective-permute-start.13 = (bf16[160,640]{1,0:T(8,128)(2,1)S(1)}, bf16[160,640]{1,0:T(8,128)(2,1)S(1)}, u32[]{:S(2)}, u32[]{:S(2)}) collective-permute-start(bf16[160,640]{1,0:T(8,128)(2,1)S(1)} %get-tuple-element.14.refs_8_), channel_id=1, source_target_pairs={{0,6},{2,0},{4,2},{6,4},{1,7},{3,1},{5,3},{7,5},{8,14},{10,8},{12,... | collective-permute-start | bytes 614408 | tf_op jit(solution)/shard_map/ppermute | solution.py:22
  92.0 2.3 %collective-permute-start.14 = (bf16[160,640]{1,0:T(8,128)(2,1)S(1)}, bf16[160,640]{1,0:T(8,128)(2,1)S(1)}, u32[]{:S(2)}, u32[]{:S(2)}) collective-permute-start(bf16[160,640]{1,0:T(8,128)(2,1)S(1)} %get-tuple-element.14.refs_8_), channel_id=1, source_target_pairs={{0,4},{2,6},{4,0},{6,2},{1,5},{3,7},{5,1},{7,3},{8,12},{10,14},{12... | collective-permute-start | bytes 614408 | tf_op jit(solution)/shard_map/ppermute | solution.py:22
  95.0 3.0 %collective-permute-done.10.refs_6_ = bf16[160,640]{1,0:T(8,128)(2,1)S(1)} collective-permute-done((bf16[160,640]{1,0:T(8,128)(2,1)}, bf16[160,640]{1,0:T(8,128)(2,1)S(1)}, u32[]{:S(2)}, u32[]{:S(2)}) %collective-permute-start.10) | collective-permute-done | bytes 204832 | tf_op jit(solution)/shard_map/ppermute | solution.py:22
  98.0 3.6 %collective-permute-start.16 = (bf16[160,640]{1,0:T(8,128)(2,1)}, bf16[160,640]{1,0:T(8,128)(2,1)S(1)}, u32[]{:S(2)}, u32[]{:S(2)}) collective-permute-start(bf16[160,640]{1,0:T(8,128)(2,1)} %get-tuple-element.15.refs_12_), channel_id=1, source_target_pairs={{0,6},{2,0},{4,2},{6,4},{1,7},{3,1},{5,3},{7,5},{8,14},{10,8},{12,... | collective-permute-start | bytes 614408 | tf_op jit(solution)/shard_map/ppermute | solution.py:22
  101.6 1.6 collective-permute-start.17
  103.1 3.5 %collective-permute-done.13.refs_10_ = bf16[160,640]{1,0:T(8,128)(2,1)S(1)} collective-permute-done((bf16[160,640]{1,0:T(8,128)(2,1)S(1)}, bf16[160,640]{1,0:T(8,128)(2,1)S(1)}, u32[]{:S(2)}, u32[]{:S(2)}) %collective-permute-start.13) | collective-permute-done | bytes 204832 | tf_op jit(solution)/shard_map/ppermute | solution.py:22
  106.6 3.7 %collective-permute-start.19 = (bf16[160,640]{1,0:T(8,128)(2,1)}, bf16[160,640]{1,0:T(8,128)(2,1)S(1)}, u32[]{:S(2)}, u32[]{:S(2)}) collective-permute-start(bf16[160,640]{1,0:T(8,128)(2,1)} %get-tuple-element.16.refs_16_), channel_id=1, source_target_pairs={{0,6},{2,0},{4,2},{6,4},{1,7},{3,1},{5,3},{7,5},{8,14},{10,8},{12,... | collective-permute-start | bytes 614408 | tf_op jit(solution)/shard_map/ppermute | solution.py:22
  110.7 1.2 collective-permute-start.20
  111.9 3.6 %collective-permute-done.16.refs_14_ = bf16[160,640]{1,0:T(8,128)(2,1)S(1)} collective-permute-done((bf16[160,640]{1,0:T(8,128)(2,1)}, bf16[160,640]{1,0:T(8,128)(2,1)S(1)}, u32[]{:S(2)}, u32[]{:S(2)}) %collective-permute-start.16) | collective-permute-done | bytes 204832 | tf_op jit(solution)/shard_map/ppermute | solution.py:22
  115.6 3.8 %collective-permute-done.18.refs_17_ = bf16[160,640]{1,0:T(8,128)(2,1)S(1)} collective-permute-done((bf16[160,640]{1,0:T(8,128)(2,1)}, bf16[160,640]{1,0:T(8,128)(2,1)S(1)}, u32[]{:S(2)}, u32[]{:S(2)}) %collective-permute-start.18) | collective-permute-done | bytes 204832 | tf_op jit(solution)/shard_map/ppermute | solution.py:22
  119.5 4.4 %collective-permute-done.19.refs_18_ = bf16[160,640]{1,0:T(8,128)(2,1)S(1)} collective-permute-done((bf16[160,640]{1,0:T(8,128)(2,1)}, bf16[160,640]{1,0:T(8,128)(2,1)S(1)}, u32[]{:S(2)}, u32[]{:S(2)}) %collective-permute-start.19) | collective-permute-done | bytes 204832 | tf_op jit(solution)/shard_map/ppermute | solution.py:22
  124.0 3.7 %collective-permute-done.9.refs_5_ = bf16[160,640]{1,0:T(8,128)(2,1)} collective-permute-done((bf16[160,640]{1,0:T(8,128)(2,1)}, bf16[160,640]{1,0:T(8,128)(2,1)}, u32[]{:S(2)}, u32[]{:S(2)}) %collective-permute-start.9) | collective-permute-done | bytes 204832 | tf_op jit(solution)/shard_map/ppermute | solution.py:22
  127.7 1.1 copy-done.4
  129.8 7.9 %left.1 = (bf16[160,640]{1,0:T(8,128)(2,1)S(1)}, bf16[160,640]{1,0:T(8,128)(2,1)S(1)}, bf16[160,640]{1,0:T(8,128)(2,1)S(1)}, bf16[160,640]{1,0:T(8,128)(2,1)S(1)}) custom-call(s32[16]{0:T(128)S(1)} %stack.102.at_ref, bf16[160,2560]{1,0:T(8,128)(2,1)S(1)} %bitcast.45, bf16[160,2560]{1,0:T(8,128)(2,1)S(1)} %copy-done.4, ...), custom_call_target="tpu_custom_call" | custom-call | flops 2097152000 | bytes 6553600 | tf_op jit(solution)/shard_map/left/pallas_call | solution.py:153
  138.7 2.5 %collective-permute-start.23 = (bf16[160,640]{1,0:T(8,128)(2,1)S(1)}, bf16[160,640]{1,0:T(8,128)(2,1)S(1)}, u32[]{:S(2)}, u32[]{:S(2)}) collective-permute-start(bf16[160,640]{1,0:T(8,128)(2,1)S(1)} %get-tuple-element.20), channel_id=1, source_target_pairs={{0,9},{1,8},{8,1},{9,0},{2,11},{3,10},{10,3},{11,2},{4,13},{5,12},... | collective-permute-start | bytes 614408 | tf_op jit(solution)/shard_map/ppermute | solution.py:201
  141.3 6.0 %collective-permute-done.22.refs_2_ = bf16[160,640]{1,0:T(8,128)(2,1)S(1)} collective-permute-done((bf16[160,640]{1,0:T(8,128)(2,1)S(1)}, bf16[160,640]{1,0:T(8,128)(2,1)S(1)}, u32[]{:S(2)}, u32[]{:S(2)}) %collective-permute-start.22) | collective-permute-done | bytes 204832 | tf_op jit(solution)/shard_map/ppermute | solution.py:22
  147.3 3.4 %collective-permute-done.23.refs_3_ = bf16[160,640]{1,0:T(8,128)(2,1)S(1)} collective-permute-done((bf16[160,640]{1,0:T(8,128)(2,1)S(1)}, bf16[160,640]{1,0:T(8,128)(2,1)S(1)}, u32[]{:S(2)}, u32[]{:S(2)}) %collective-permute-start.23) | collective-permute-done | bytes 204832 | tf_op jit(solution)/shard_map/ppermute | solution.py:201
  150.7 2.6 %pack.3 = bf16[640,640]{1,0:T(8,128)(2,1)} custom-call(s32[1,160]{1,0:T(1,128)S(1)} %fusion.10.base_ref, s32[4]{0:T(128)S(1)} %pad_add_fusion.part_ref, bf16[160,640]{1,0:T(8,128)(2,1)S(1)} %get-tuple-element.17.refs_0_, bf16[160,640]{1,0:T(8,128)(2,1)S(1)} %collective-permute-done.21.refs_1_, bf16[160,640]{1,0:T(8,128)(2,1)S(1)} %collective-permute-done.22.refs_2_, ...), custom_call_target="tpu_custom_call" | custom-call | tf_op jit(solution)/shard_map/pack/pallas_call | solution.py:61
  153.4 7.1 %all-to-all-start.1 = ((bf16[16,40,640]{2,1,0:T(8,128)(2,1)}), bf16[16,40,640]{2,1,0:T(8,128)(2,1)S(1)}, u32[]{:S(2)}, u32[]{:S(2)}) async-start(bf16[16,40,640]{2,1,0:T(8,128)(2,1)} %bitcast.30), calls=%async_computation.1 | async-start | bytes 1638400 | tf_op jit(solution)/shard_map/all_to_all | solution.py:179
  160.6 21.8 %all-to-all-done.1 = bf16[16,40,640]{2,1,0:T(8,128)(2,1)S(1)} async-done(((bf16[16,40,640]{2,1,0:T(8,128)(2,1)}), bf16[16,40,640]{2,1,0:T(8,128)(2,1)S(1)}, u32[]{:S(2)}, u32[]{:S(2)}) %all-to-all-start.1) | async-done | bytes 819232 | tf_op jit(solution)/shard_map/all_to_all | solution.py:179
  182.4 1.9 %unpack.3 = bf16[160,2560]{1,0:T(8,128)(2,1)} custom-call(s32[160,1]{1,0:T(8,128)S(1)} %fusion.6.base_ref, bf16[640,640]{1,0:T(8,128)(2,1)S(1)} %bitcast.37), custom_call_target="tpu_custom_call" | custom-call | tf_op jit(solution)/shard_map/unpack/pallas_call | solution.py:89
  (54 shorter events, 9.3 us)
Async XLA Ops:
  0.8 1.1 copy-start
  4.5 9.6 %copy-start.1 = (bf16[1,160,2560]{2,1,0:T(8,128)(2,1)S(1)}, bf16[1,160,2560]{2,1,0:T(8,128)(2,1)}, u32[]{:S(2)}) copy-start(bf16[1,160,2560]{2,1,0:T(8,128)(2,1)} %param.7) | copy-start | bytes 2457604
  4.5 31.1 %all-to-all-start = ((bf16[16,40,640]{2,1,0:T(8,128)(2,1)}), bf16[16,40,640]{2,1,0:T(8,128)(2,1)S(1)}, u32[]{:S(2)}, u32[]{:S(2)}) async-start(bf16[16,40,640]{2,1,0:T(8,128)(2,1)} %bitcast.27), calls=%async_computation | async-start | bytes 1638400 | tf_op jit(solution)/shard_map/all_to_all | solution.py:179
  14.2 29.7 %collective-permute-start.6 = (bf16[160,2560]{1,0:T(8,128)(2,1)S(1)}, bf16[160,2560]{1,0:T(8,128)(2,1)}, u32[]{:S(2)}, u32[]{:S(2)}) collective-permute-start(bf16[160,2560]{1,0:T(8,128)(2,1)S(1)} %bitcast.39), channel_id=1, source_target_pairs={{0,2},{2,4},{4,6},{6,0},{1,3},{3,5},{5,7},{7,1},{8,10},{10,12},{12... | collective-permute-start | bytes 2457608 | tf_op jit(solution)/shard_map/ppermute | solution.py:22
  35.6 6.8 %copy-start.2 = (bf16[1,160,2560]{2,1,0:T(8,128)(2,1)S(1)}, bf16[1,160,2560]{2,1,0:T(8,128)(2,1)}, u32[]{:S(2)}) copy-start(bf16[1,160,2560]{2,1,0:T(8,128)(2,1)} %param.6) | copy-start | bytes 2457604
  36.6 22.9 %collective-permute-start.4 = (bf16[160,2560]{1,0:T(8,128)(2,1)S(1)}, bf16[160,2560]{1,0:T(8,128)(2,1)}, u32[]{:S(2)}, u32[]{:S(2)}) collective-permute-start(bf16[160,2560]{1,0:T(8,128)(2,1)S(1)} %unpack.2.refs_0_), channel_id=1, source_target_pairs={{0,8},{8,0},{1,9},{9,1},{2,10},{10,2},{3,11},{11,3},{4,12},{12,4},... | collective-permute-start | bytes 2457608 | tf_op jit(solution)/shard_map/ppermute | solution.py:22
  39.4 35.4 %collective-permute-start.7 = (bf16[160,2560]{1,0:T(8,128)(2,1)S(1)}, bf16[160,2560]{1,0:T(8,128)(2,1)S(1)}, u32[]{:S(2)}, u32[]{:S(2)}) collective-permute-start(bf16[160,2560]{1,0:T(8,128)(2,1)S(1)} %bitcast.40), channel_id=1, source_target_pairs={{0,6},{2,0},{4,2},{6,4},{1,7},{3,1},{5,3},{7,5},{8,14},{10,8},{12,... | collective-permute-start | bytes 2457608 | tf_op jit(solution)/shard_map/ppermute | solution.py:22
  42.4 32.4 %collective-permute-start.1 = (bf16[160,2560]{1,0:T(8,128)(2,1)S(1)}, bf16[160,2560]{1,0:T(8,128)(2,1)}, u32[]{:S(2)}, u32[]{:S(2)}) collective-permute-start(bf16[160,2560]{1,0:T(8,128)(2,1)S(1)} %bitcast.43), channel_id=1, source_target_pairs={{0,8},{8,0},{1,9},{9,1},{2,10},{10,2},{3,11},{11,3},{4,12},{12,4},... | collective-permute-start | bytes 2457608 | tf_op jit(solution)/shard_map/ppermute | solution.py:22
  43.2 32.5 %collective-permute-start.8 = (bf16[160,2560]{1,0:T(8,128)(2,1)S(1)}, bf16[160,2560]{1,0:T(8,128)(2,1)}, u32[]{:S(2)}, u32[]{:S(2)}) collective-permute-start(bf16[160,2560]{1,0:T(8,128)(2,1)S(1)} %bitcast.41), channel_id=1, source_target_pairs={{0,4},{2,6},{4,0},{6,2},{1,5},{3,7},{5,1},{7,3},{8,12},{10,14},{12... | collective-permute-start | bytes 2457608 | tf_op jit(solution)/shard_map/ppermute | solution.py:22
  43.9 31.9 %collective-permute-start.3 = (bf16[160,2560]{1,0:T(8,128)(2,1)S(1)}, bf16[160,2560]{1,0:T(8,128)(2,1)}, u32[]{:S(2)}, u32[]{:S(2)}) collective-permute-start(bf16[160,2560]{1,0:T(8,128)(2,1)S(1)} %unpack.2.refs_0_), channel_id=1, source_target_pairs={{0,1},{1,0},{2,3},{3,2},{4,5},{5,4},{6,7},{7,6},{8,9},{9,8},{10,11... | collective-permute-start | bytes 2457608 | tf_op jit(solution)/shard_map/ppermute | solution.py:22
  59.5 16.3 %collective-permute-start.5 = (bf16[160,2560]{1,0:T(8,128)(2,1)}, bf16[160,2560]{1,0:T(8,128)(2,1)}, u32[]{:S(2)}, u32[]{:S(2)}) collective-permute-start(bf16[160,2560]{1,0:T(8,128)(2,1)} %collective-permute-done.4.refs_2_), channel_id=1, source_target_pairs={{0,1},{1,0},{2,3},{3,2},{4,5},{5,4},{6,7},{7,6},{8,9},{9,8},{10,11... | collective-permute-start | bytes 2457608 | tf_op jit(solution)/shard_map/ppermute | solution.py:22
  74.8 14.0 %collective-permute-start = (bf16[160,2560]{1,0:T(8,128)(2,1)S(1)}, bf16[160,2560]{1,0:T(8,128)(2,1)S(1)}, u32[]{:S(2)}, u32[]{:S(2)}) collective-permute-start(bf16[160,2560]{1,0:T(8,128)(2,1)S(1)} %bitcast.44), channel_id=1, source_target_pairs={{0,1},{1,0},{2,3},{3,2},{4,5},{5,4},{6,7},{7,6},{8,9},{9,8},{10,11... | collective-permute-start | bytes 2457608 | tf_op jit(solution)/shard_map/ppermute | solution.py:22
  75.7 16.3 %collective-permute-start.2 = (bf16[160,2560]{1,0:T(8,128)(2,1)}, bf16[160,2560]{1,0:T(8,128)(2,1)}, u32[]{:S(2)}, u32[]{:S(2)}) collective-permute-start(bf16[160,2560]{1,0:T(8,128)(2,1)} %collective-permute-done.1.refs_2_), channel_id=1, source_target_pairs={{0,1},{1,0},{2,3},{3,2},{4,5},{5,4},{6,7},{7,6},{8,9},{9,8},{10,11... | collective-permute-start | bytes 2457608 | tf_op jit(solution)/shard_map/ppermute | solution.py:22
  84.1 13.9 %collective-permute-start.10 = (bf16[160,640]{1,0:T(8,128)(2,1)}, bf16[160,640]{1,0:T(8,128)(2,1)S(1)}, u32[]{:S(2)}, u32[]{:S(2)}) collective-permute-start(bf16[160,640]{1,0:T(8,128)(2,1)} %get-tuple-element.13.refs_4_), channel_id=1, source_target_pairs={{0,6},{2,0},{4,2},{6,4},{1,7},{3,1},{5,3},{7,5},{8,14},{10,8},{12,... | collective-permute-start | bytes 614408 | tf_op jit(solution)/shard_map/ppermute | solution.py:22
  87.9 10.1 %collective-permute-start.11 = (bf16[160,640]{1,0:T(8,128)(2,1)}, bf16[160,640]{1,0:T(8,128)(2,1)S(1)}, u32[]{:S(2)}, u32[]{:S(2)}) collective-permute-start(bf16[160,640]{1,0:T(8,128)(2,1)} %get-tuple-element.13.refs_4_), channel_id=1, source_target_pairs={{0,4},{2,6},{4,0},{6,2},{1,5},{3,7},{5,1},{7,3},{8,12},{10,14},{12... | collective-permute-start | bytes 614408 | tf_op jit(solution)/shard_map/ppermute | solution.py:22
  87.9 13.7 %collective-permute-start.12 = (bf16[160,640]{1,0:T(8,128)(2,1)S(1)}, bf16[160,640]{1,0:T(8,128)(2,1)S(1)}, u32[]{:S(2)}, u32[]{:S(2)}) collective-permute-start(bf16[160,640]{1,0:T(8,128)(2,1)S(1)} %get-tuple-element.14.refs_8_), channel_id=1, source_target_pairs={{0,2},{2,4},{4,6},{6,0},{1,3},{3,5},{5,7},{7,1},{8,10},{10,12},{12... | collective-permute-start | bytes 614408 | tf_op jit(solution)/shard_map/ppermute | solution.py:22
  88.8 0.9 copy-start.3
  89.7 16.9 %collective-permute-start.13 = (bf16[160,640]{1,0:T(8,128)(2,1)S(1)}, bf16[160,640]{1,0:T(8,128)(2,1)S(1)}, u32[]{:S(2)}, u32[]{:S(2)}) collective-permute-start(bf16[160,640]{1,0:T(8,128)(2,1)S(1)} %get-tuple-element.14.refs_8_), channel_id=1, source_target_pairs={{0,6},{2,0},{4,2},{6,4},{1,7},{3,1},{5,3},{7,5},{8,14},{10,8},{12,... | collective-permute-start | bytes 614408 | tf_op jit(solution)/shard_map/ppermute | solution.py:22
  92.0 14.6 %collective-permute-start.14 = (bf16[160,640]{1,0:T(8,128)(2,1)S(1)}, bf16[160,640]{1,0:T(8,128)(2,1)S(1)}, u32[]{:S(2)}, u32[]{:S(2)}) collective-permute-start(bf16[160,640]{1,0:T(8,128)(2,1)S(1)} %get-tuple-element.14.refs_8_), channel_id=1, source_target_pairs={{0,4},{2,6},{4,0},{6,2},{1,5},{3,7},{5,1},{7,3},{8,12},{10,14},{12... | collective-permute-start | bytes 614408 | tf_op jit(solution)/shard_map/ppermute | solution.py:22
  98.0 12.7 %collective-permute-start.15 = (bf16[160,640]{1,0:T(8,128)(2,1)}, bf16[160,640]{1,0:T(8,128)(2,1)S(1)}, u32[]{:S(2)}, u32[]{:S(2)}) collective-permute-start(bf16[160,640]{1,0:T(8,128)(2,1)} %get-tuple-element.15.refs_12_), channel_id=1, source_target_pairs={{0,2},{2,4},{4,6},{6,0},{1,3},{3,5},{5,7},{7,1},{8,10},{10,12},{12... | collective-permute-start | bytes 614408 | tf_op jit(solution)/shard_map/ppermute | solution.py:22
  98.0 17.5 %collective-permute-start.16 = (bf16[160,640]{1,0:T(8,128)(2,1)}, bf16[160,640]{1,0:T(8,128)(2,1)S(1)}, u32[]{:S(2)}, u32[]{:S(2)}) collective-permute-start(bf16[160,640]{1,0:T(8,128)(2,1)} %get-tuple-element.15.refs_12_), channel_id=1, source_target_pairs={{0,6},{2,0},{4,2},{6,4},{1,7},{3,1},{5,3},{7,5},{8,14},{10,8},{12,... | collective-permute-start | bytes 614408 | tf_op jit(solution)/shard_map/ppermute | solution.py:22
  101.6 14.1 %collective-permute-start.17 = (bf16[160,640]{1,0:T(8,128)(2,1)}, bf16[160,640]{1,0:T(8,128)(2,1)S(1)}, u32[]{:S(2)}, u32[]{:S(2)}) collective-permute-start(bf16[160,640]{1,0:T(8,128)(2,1)} %get-tuple-element.15.refs_12_), channel_id=1, source_target_pairs={{0,4},{2,6},{4,0},{6,2},{1,5},{3,7},{5,1},{7,3},{8,12},{10,14},{12... | collective-permute-start | bytes 614408 | tf_op jit(solution)/shard_map/ppermute | solution.py:22
  106.6 12.8 %collective-permute-start.18 = (bf16[160,640]{1,0:T(8,128)(2,1)}, bf16[160,640]{1,0:T(8,128)(2,1)S(1)}, u32[]{:S(2)}, u32[]{:S(2)}) collective-permute-start(bf16[160,640]{1,0:T(8,128)(2,1)} %get-tuple-element.16.refs_16_), channel_id=1, source_target_pairs={{0,2},{2,4},{4,6},{6,0},{1,3},{3,5},{5,7},{7,1},{8,10},{10,12},{12... | collective-permute-start | bytes 614408 | tf_op jit(solution)/shard_map/ppermute | solution.py:22
  106.6 17.3 %collective-permute-start.19 = (bf16[160,640]{1,0:T(8,128)(2,1)}, bf16[160,640]{1,0:T(8,128)(2,1)S(1)}, u32[]{:S(2)}, u32[]{:S(2)}) collective-permute-start(bf16[160,640]{1,0:T(8,128)(2,1)} %get-tuple-element.16.refs_16_), channel_id=1, source_target_pairs={{0,6},{2,0},{4,2},{6,4},{1,7},{3,1},{5,3},{7,5},{8,14},{10,8},{12,... | collective-permute-start | bytes 614408 | tf_op jit(solution)/shard_map/ppermute | solution.py:22
  110.7 13.3 %collective-permute-start.20 = (bf16[160,640]{1,0:T(8,128)(2,1)}, bf16[160,640]{1,0:T(8,128)(2,1)S(1)}, u32[]{:S(2)}, u32[]{:S(2)}) collective-permute-start(bf16[160,640]{1,0:T(8,128)(2,1)} %get-tuple-element.16.refs_16_), channel_id=1, source_target_pairs={{0,4},{2,6},{4,0},{6,2},{1,5},{3,7},{5,1},{7,3},{8,12},{10,14},{12... | collective-permute-start | bytes 614408 | tf_op jit(solution)/shard_map/ppermute | solution.py:22
  115.5 12.2 %collective-permute-start.9 = (bf16[160,640]{1,0:T(8,128)(2,1)}, bf16[160,640]{1,0:T(8,128)(2,1)}, u32[]{:S(2)}, u32[]{:S(2)}) collective-permute-start(bf16[160,640]{1,0:T(8,128)(2,1)} %get-tuple-element.13.refs_4_), channel_id=1, source_target_pairs={{0,2},{2,4},{4,6},{6,0},{1,3},{3,5},{5,7},{7,1},{8,10},{10,12},{12... | collective-permute-start | bytes 614408 | tf_op jit(solution)/shard_map/ppermute | solution.py:22
  127.7 1.1 copy-start.4
  128.9 0.9 copy-start.6
  137.7 3.6 %collective-permute-start.21 = (bf16[160,640]{1,0:T(8,128)(2,1)S(1)}, bf16[160,640]{1,0:T(8,128)(2,1)S(1)}, u32[]{:S(2)}, u32[]{:S(2)}) collective-permute-start(bf16[160,640]{1,0:T(8,128)(2,1)S(1)} %get-tuple-element.18), channel_id=1, source_target_pairs={{0,1},{1,0},{2,3},{3,2},{4,5},{5,4},{6,7},{7,6},{8,9},{9,8},{10,11... | collective-permute-start | bytes 614408 | tf_op jit(solution)/shard_map/ppermute | solution.py:22
  137.8 9.5 %collective-permute-start.22 = (bf16[160,640]{1,0:T(8,128)(2,1)S(1)}, bf16[160,640]{1,0:T(8,128)(2,1)S(1)}, u32[]{:S(2)}, u32[]{:S(2)}) collective-permute-start(bf16[160,640]{1,0:T(8,128)(2,1)S(1)} %get-tuple-element.19), channel_id=1, source_target_pairs={{0,8},{8,0},{1,9},{9,1},{2,10},{10,2},{3,11},{11,3},{4,12},{12,4},... | collective-permute-start | bytes 614408 | tf_op jit(solution)/shard_map/ppermute | solution.py:22
  138.7 12.0 %collective-permute-start.23 = (bf16[160,640]{1,0:T(8,128)(2,1)S(1)}, bf16[160,640]{1,0:T(8,128)(2,1)S(1)}, u32[]{:S(2)}, u32[]{:S(2)}) collective-permute-start(bf16[160,640]{1,0:T(8,128)(2,1)S(1)} %get-tuple-element.20), channel_id=1, source_target_pairs={{0,9},{1,8},{8,1},{9,0},{2,11},{3,10},{10,3},{11,2},{4,13},{5,12},... | collective-permute-start | bytes 614408 | tf_op jit(solution)/shard_map/ppermute | solution.py:201
  153.4 29.0 %all-to-all-start.1 = ((bf16[16,40,640]{2,1,0:T(8,128)(2,1)}), bf16[16,40,640]{2,1,0:T(8,128)(2,1)S(1)}, u32[]{:S(2)}, u32[]{:S(2)}) async-start(bf16[16,40,640]{2,1,0:T(8,128)(2,1)} %bitcast.30), calls=%async_computation.1 | async-start | bytes 1638400 | tf_op jit(solution)/shard_map/all_to_all | solution.py:179
  (2 other events, 1.6 us)

commit v2 on v0

v2 whole, which is shorter than its diff:
```python
import functools

import jax
import jax.numpy as jnp
from jax import lax
from jax.experimental import pallas as pl
from jax.experimental.pallas import tpu as pltpu
from jax.sharding import Mesh, PartitionSpec as P

AXES = ("xl", "z", "xh", "y", "c")
SIZES = dict(xl=2, z=8, xh=2, y=4, c=2)
DP = ("xl", "z")
NEAR = ("xh", "c")
LAYERS = 16
ROWS = 10
BLOCK = ROWS * LAYERS
PARTS = 4
WIDE = 2560
COLS = WIDE // PARTS
F32 = jnp.float32
BF16 = jnp.bfloat16

TO, PART, BAT, RAT, SIDE = 0, 16, 20, 25, 41


def shift(value, axis, by):
    n = SIZES[axis]
    return lax.ppermute(value, axis, [(i, (i + by) % n) for i in range(n)])


def flip(value, mask):
    return lax.ppermute(value, NEAR, [(i, i ^ mask) for i in range(4)])


def params(mib):
    return pltpu.CompilerParams(vmem_limit_bytes=mib * 1024 * 1024)


def cost(flops, size):
    return pl.CostEstimate(flops=flops, bytes_accessed=size, transcendentals=0)


SMEM = pl.BlockSpec(memory_space=pltpu.SMEM)
VMEM = pl.BlockSpec(memory_space=pltpu.VMEM)


def onehot(hit):
    return jnp.where(hit, 1.0, 0.0).astype(BF16)


def first_row(meta, by_layer, m):
    if not by_layer:
        return lax.div(m, ROWS) * (PARTS * ROWS) + lax.rem(m, ROWS)
    total = lax.div(m, LAYERS)
    layer = lax.rem(m, LAYERS)
    for n in range(LAYERS):
        total = total + jnp.where(layer == n, meta[TO + n], 0)
    return total


def pack_kernel(by_layer, meta, *refs):
    x_refs, o_ref = refs[:-1], refs[-1]
    base = first_row(meta, by_layer, lax.broadcasted_iota(jnp.int32, (1, BLOCK), 1))
    row = lax.broadcasted_iota(jnp.int32, (PARTS * BLOCK, BLOCK), 0)
    total = None
    for q in range(PARTS):
        x = x_refs[q][...] if len(x_refs) > 1 else x_refs[0][:, q * COLS : (q + 1) * COLS]
        part = meta[PART + q] if len(x_refs) > 1 else q
        term = jnp.dot(onehot(row == base + ROWS * part), x, preferred_element_type=F32)
        total = term if total is None else total + term
    o_ref[...] = total.astype(BF16)


def pack(meta, by_layer, xs):
    return pl.pallas_call(
        functools.partial(pack_kernel, by_layer),
        out_shape=jax.ShapeDtypeStruct((PARTS * BLOCK, COLS), BF16),
        in_specs=[SMEM] + [VMEM] * len(xs),
        out_specs=VMEM,
        compiler_params=params(8),
        cost_estimate=cost(2 * BLOCK * BLOCK * WIDE * 4, 4 * BLOCK * WIDE),
        name="pack",
    )(meta, *xs)


def unpack_kernel(by_layer, interleave, meta, x_ref, o_ref):
    base = first_row(meta, by_layer, lax.broadcasted_iota(jnp.int32, (BLOCK, 1), 0))
    col = lax.broadcasted_iota(jnp.int32, (BLOCK, PARTS * BLOCK), 1)
    for q in range(PARTS):
        block = jnp.dot(onehot(col == base + ROWS * q), x_ref[...], preferred_element_type=F32).astype(BF16)
        if not interleave:
            o_ref[:, q * COLS : (q + 1) * COLS] = block
            continue
        xh, c = q // 2, q % 2
        for y in range(4):
            at = (xh * 8 + y * 2 + c) * BLOCK
            o_ref[:, at : at + BLOCK] = block[:, y * BLOCK : (y + 1) * BLOCK]


def unpack(meta, by_layer, interleave, x):
    return pl.pallas_call(
        functools.partial(unpack_kernel, by_layer, interleave),
        out_shape=jax.ShapeDtypeStruct((BLOCK, WIDE), BF16),
        in_specs=[SMEM, VMEM],
        out_specs=VMEM,
        compiler_params=params(8),
        cost_estimate=cost(2 * BLOCK * BLOCK * WIDE * 4, 4 * BLOCK * WIDE),
        name="unpack",
    )(meta, x)


def place_kernel(meta, *refs):
    x_refs, (o_ref, sem) = refs[:-2], refs[-2:]
    copies = [
        pltpu.make_async_copy(x, o_ref.at[pl.ds(pl.multiple_of(meta[BAT + n], 16), x.shape[0])], sem.at[n])
        for n, x in enumerate(x_refs)
    ]
    for copy in copies:
        copy.start()
    for copy in copies:
        copy.wait()


def place(meta, xs):
    rows = sum(x.shape[0] for x in xs)
    return pl.pallas_call(
        place_kernel,
        out_shape=jax.ShapeDtypeStruct((rows, WIDE), BF16),
        in_specs=[SMEM] + [pl.BlockSpec(memory_space=pltpu.HBM)] * len(xs),
        out_specs=VMEM,
        scratch_shapes=[pltpu.SemaphoreType.DMA((len(xs),))],
        compiler_params=params(4),
        cost_estimate=cost(10000000000, 4 * rows * WIDE),
        name="place",
    )(meta, *xs)


def right_kernel(count, b_ref, *refs):
    g_refs, (o, g_all) = refs[:count], refs[count:]
    for n, g in enumerate(g_refs):
        g_all[n * BLOCK : (n + 1) * BLOCK] = g[...]
    o[...] = lax.dot_general(
        g_all[...], b_ref[...], (((1,), (1,)), ((), ())), preferred_element_type=F32
    ).astype(BF16)


def right(gs, b):
    n = len(gs)
    return pl.pallas_call(
        functools.partial(right_kernel, n),
        out_shape=jax.ShapeDtypeStruct((n * BLOCK, COLS), BF16),
        in_specs=[VMEM] + [VMEM] * n,
        out_specs=VMEM,
        scratch_shapes=[pltpu.VMEM((n * BLOCK, WIDE), BF16)],
        compiler_params=params(8),
        cost_estimate=cost(2 * n * BLOCK * COLS * WIDE, 2 * (n * BLOCK + COLS) * WIDE),
        name="right",
    )(b, *gs)


def left_kernel(side, meta, *refs):
    a_refs, r_refs = refs[:4], refs[4:8]
    a_all, r_all = refs[-2:]
    columns = pl.ds(pl.multiple_of(meta[SIDE + side], 128), WIDE // 2)
    for n, a in enumerate(a_refs):
        a_all[n * BLOCK : (n + 1) * BLOCK] = a[:, columns]
    for n, r in enumerate(r_refs):
        for k in range(2):
            to = pl.ds(pl.multiple_of(meta[RAT + 8 * side + 2 * n + k], 16), BLOCK)
            r_all[to] = r[k * BLOCK : (k + 1) * BLOCK]
    total = jnp.dot(a_all[...], r_all[...], preferred_element_type=F32)
    if side == 0:
        refs[8][...] = total
        return
    total = (total + refs[8][...]).astype(BF16)
    for n, o in enumerate(refs[9:13]):
        o[...] = total[n * BLOCK : (n + 1) * BLOCK]


def left(meta, side, blocks, rs, partial=None):
    first = side == 0
    return pl.pallas_call(
        functools.partial(left_kernel, side),
        out_shape=jax.ShapeDtypeStruct((COLS, COLS), F32)
        if first
        else [jax.ShapeDtypeStruct((BLOCK, COLS), BF16)] * 4,
        in_specs=[SMEM] + [VMEM] * 8 + ([] if first else [VMEM]),
        out_specs=VMEM if first else [VMEM] * 4,
        scratch_shapes=[
            pltpu.VMEM((COLS, WIDE // 2), BF16),
            pltpu.VMEM((WIDE // 2, COLS), BF16),
        ],
        compiler_params=params(10),
        cost_estimate=cost(COLS * COLS * WIDE, 4 * COLS * WIDE),
        name="left",
    )(meta, *blocks, *rs, *([] if first else [partial]))


def along_y(value):
    return [value, shift(value, "y", 1), shift(value, "y", -1), shift(value, "y", 2)]


def exchange(x):
    x = x.reshape(LAYERS, PARTS * ROWS, COLS)
    return lax.all_to_all(x, DP, split_axis=0, concat_axis=0, tiled=True).reshape(-1, COLS)


def after(value, *others):
    return lax.optimization_barrier((value, others))[0]


def local(gradient, owner, a_inverse, b_inverse):
    xh, y, c = (lax.axis_index(n) for n in ("xh", "y", "c"))
    a, b = a_inverse[0], b_inverse[0]
    ys = [y, (y + 3) % 4, (y + 1) % 4, (y + 2) % 4]
    near = [(xh, c), (xh, 1 - c), (1 - xh, c), (1 - xh, 1 - c)]
    scalars = [u * 2 + w for u, w in near]
    scalars += [v * BLOCK for v in ys] + [ys[3] * BLOCK + BLOCK // 2]
    scalars += [(v * 2 + w) * BLOCK for v in ys for w in (c, 1 - c)] * 2
    scalars += [xh * (WIDE // 2), (1 - xh) * (WIDE // 2)]
    meta = jnp.concatenate([owner * (PARTS * ROWS), jnp.stack(scalars)]).astype(jnp.int32)

    half = BLOCK // 2
    up, down = shift(b, "y", 1), shift(b, "y", -1)
    bs = [b, up, down, shift(up[:half], "y", 1), shift(down[half:], "y", -1)]
    rows = gradient.transpose(1, 0, 2).reshape(BLOCK, WIDE)
    packed = pack(meta, True, [rows])
    a = after(a, packed)
    over = flip(a, 2)
    blocks = [a, flip(a, 1), over, flip(over, 1)]
    got, b, blocks = lax.optimization_barrier((exchange(packed), place(meta, bs), blocks))
    g = unpack(meta, False, False, got)
    over = flip(g, 2)
    r = right([g, flip(g, 1)], b)
    first = along_y(r)
    over = after(over, first)
    second = along_y(right([over, flip(over, 1)], b))
    partial = left(meta, 0, blocks, first)
    out = left(meta, 1, blocks, second, partial)
    mine = [out[0]] + [flip(out[mask], mask) for mask in range(1, 4)]
    done = unpack(meta, True, True, exchange(pack(meta, False, mine)))
    return done.reshape(ROWS, LAYERS, WIDE).transpose(1, 0, 2)


def solution(mesh):
    fine = Mesh(mesh.devices.reshape(tuple(SIZES[n] for n in AXES)), AXES)
    rows = ("xh", "y", "c")
    in_specs = (P(None, rows + DP, None), P(), P(DP, rows, None), P(DP, rows, None))
    return jax.shard_map(
        local, mesh=fine, in_specs=in_specs, out_specs=P(None, rows + DP, None), check_vma=False
    )
```

time: 282 us -> 150 us (0.53)
  waiting for transfers between devices: 185 us -> 57.5 us
  starting transfers between devices: 7.54 us -> 34 us
  Pallas kernels: 0 us -> 19.6 us
  matrix products: 15.9 us -> 0 us
  between operations: 13.5 us -> 0.13 us
  blocking collectives: 42.1 us -> 32.2 us
  local copies, waits for them, and re-layouts: 11.9 us -> 5.63 us
  other arithmetic: 5.81 us -> 0.66 us
    all_gather x2 -> x0, waiting for transfers between devices: 162 us -> none  [the longest x1 95.9 us: local(): lax.all_gather(right_half, 'shard', axis=0, tiled=True)]
    ppermute x0 -> x19, waiting for transfers between devices: none -> 57.5 us  [the longest x9 35.7 us: flip(): return lax.ppermute(value, NEAR, [(i, i ^ mask) for i in range(4)])]
    ppermute x0 -> x19, starting transfers between devices: none -> 25.4 us  [the longest x10 14.5 us: shift(): return lax.ppermute(value, axis, [(i, (i + by) % n) for i in range(n)])]
    all_to_all x1, waiting for transfers between devices: 21.8 us -> 0.01 us  [exchange(): lax.all_to_all(x, DP, split_axis=0, concat_axis=0, tiled=True)]
    pallas_call x0 -> x9, Pallas kernels: none -> 19.6 us  [the longest x2 6.46 us: left(): pl.pallas_call(functools.partial(left_kernel, side), out_shape=jax.ShapeD...]
    dot_general x3 -> x0, matrix products: 15.9 us -> none  [the longest x1 7.9 us: local(): jnp.dot(columns, lax.all_gather(right_rows, 'shard', axis=0, tiled=True),...]
    all_to_all x1, blocking collectives: 42.1 us -> 32.2 us  [exchange(): lax.all_to_all(x, DP, split_axis=0, concat_axis=0, tiled=True)]
    unnamed x1 -> x0, other arithmetic: 5.61 us -> none
  transfers between devices with their start and end apart: 3 -> 20, of which waited for: 3 -> 11; matrix products, arithmetic and copies ran while one was open for 1% -> 1% of each run, Pallas kernels for 0% -> 6%
where the time goes in v2:
time: 150 us
  waiting for transfers between devices  57.5 us (38%)
  starting transfers between devices  34 us (23%)
  blocking collectives  32.2 us (21%)
  Pallas kernels  19.6 us (13%)
  local copies, waits for them, and re-layouts  5.63 us (4%)
    ppermute x9, waiting for transfers between devices, flip(): return lax.ppermute(value, NEAR, [(i, i ^ mask) for i in range(4)])  35.7 us
    all_to_all x1, blocking collectives, exchange(): lax.all_to_all(x, DP, split_axis=0, concat_axis=0, tiled=True)  32.2 us
    ppermute x10, waiting for transfers between devices, shift(): return lax.ppermute(value, axis, [(i, (i + by) % n) for i in range(n)])  21.8 us
    ppermute x10, starting transfers between devices, shift(): return lax.ppermute(value, axis, [(i, (i + by) % n) for i in range(n)])  14.5 us
    ppermute x9, starting transfers between devices, flip(): return lax.ppermute(value, NEAR, [(i, i ^ mask) for i in range(4)])  10.9 us
    all_to_all x1, starting transfers between devices, exchange(): lax.all_to_all(x, DP, split_axis=0, concat_axis=0, tiled=True)  8.62 us
    pallas_call x2, Pallas kernels, left(): pl.pallas_call(functools.partial(left_kernel, side), out_shape=jax.ShapeD...  6.46 us
    unnamed x16, local copies, waits for them, and re-layouts  5.47 us
  transfers between devices with their start and end apart: 20, of which 11 were waited for; matrix products, arithmetic and copies ran while one was open for 1% of the time, Pallas kernels for 6%

profile of v2, /device:TPU:32, one launch (start us, length us, event | category | flops | bytes accessed | tf_op | source)
XLA Modules:
  0.0 149.7 jit_solution(17171984109550118841)
XLA Ops:
  0.0 3.0 %collective-permute-start.1 = (bf16[160,2560]{1,0:T(8,128)(2,1)}, bf16[160,2560]{1,0:T(8,128)(2,1)S(1)}, u32[]{:S(2)}, u32[]{:S(2)}) collective-permute-start(bf16[160,2560]{1,0:T(8,128)(2,1)} %bitcast.34), channel_id=1, source_target_pairs={{0,6},{2,0},{4,2},{6,4},{1,7},{3,1},{5,3},{7,5},{8,14},{10,8},{12,... | collective-permute-start | bytes 2457608 | tf_op jit(solution)/shard_map/ppermute | solution.py:28
  3.8 1.1 copy-done.6
  4.9 2.7 %pack.2 = bf16[640,640]{1,0:T(8,128)(2,1)} custom-call(s32[43]{0:T(128)S(1)} %concatenate.3.meta, bf16[160,2560]{1,0:T(8,128)(2,1)S(1)} %bitcast.33), custom_call_target="tpu_custom_call" | custom-call | flops 524288000 | bytes 1638400 | tf_op jit(solution)/shard_map/pack/pallas_call | solution.py:75
  7.6 3.0 %collective-permute-start.5 = (bf16[160,2560]{1,0:T(8,128)(2,1)}, bf16[160,2560]{1,0:T(8,128)(2,1)}, u32[]{:S(2)}, u32[]{:S(2)}) collective-permute-start(bf16[160,2560]{1,0:T(8,128)(2,1)} %bitcast.24.refs_0_), channel_id=1, source_target_pairs={{0,8},{1,9},{8,0},{9,1},{2,10},{3,11},{10,2},{11,3},{4,12},{5,13},... | collective-permute-start | bytes 2457608 | tf_op jit(solution)/shard_map/ppermute | solution.py:32
  10.6 8.6 %all-to-all-start = ((bf16[16,40,640]{2,1,0:T(8,128)(2,1)}), bf16[16,40,640]{2,1,0:T(8,128)(2,1)}, u32[]{:S(2)}, u32[]{:S(2)}) async-start(bf16[16,40,640]{2,1,0:T(8,128)(2,1)} %bitcast.21), calls=%async_computation | async-start | bytes 1638400 | tf_op jit(solution)/shard_map/all_to_all | solution.py:205
  19.2 1.6 %collective-permute-done.1.refs_2_ = bf16[160,2560]{1,0:T(8,128)(2,1)S(1)} collective-permute-done((bf16[160,2560]{1,0:T(8,128)(2,1)}, bf16[160,2560]{1,0:T(8,128)(2,1)S(1)}, u32[]{:S(2)}, u32[]{:S(2)}) %collective-permute-start.1) | collective-permute-done | bytes 819232 | tf_op jit(solution)/shard_map/ppermute | solution.py:28
  20.9 3.7 %collective-permute-start.3 = (bf16[80,2560]{1,0:T(8,128)(2,1)S(1)}, bf16[80,2560]{1,0:T(8,128)(2,1)S(1)}, u32[]{:S(2)}, u32[]{:S(2)}) collective-permute-start(bf16[80,2560]{1,0:T(8,128)(2,1)S(1)} %slice.9), channel_id=1, source_target_pairs={{0,6},{2,0},{4,2},{6,4},{1,7},{3,1},{5,3},{7,5},{8,14},{10,8},{12,... | collective-permute-start | bytes 1228808 | tf_op jit(solution)/shard_map/ppermute | solution.py:28
  24.8 10.8 %collective-permute-done.5.refs_2_ = bf16[160,2560]{1,0:T(8,128)(2,1)} collective-permute-done((bf16[160,2560]{1,0:T(8,128)(2,1)}, bf16[160,2560]{1,0:T(8,128)(2,1)}, u32[]{:S(2)}, u32[]{:S(2)}) %collective-permute-start.5) | collective-permute-done | bytes 819232 | tf_op jit(solution)/shard_map/ppermute | solution.py:32
  36.0 1.1 copy-done.3
  37.2 1.1 copy-done.5
  38.3 1.1 copy-done.7
  39.5 1.3 place.1.b_ref
  41.7 2.1 %unpack.2.refs_0_ = bf16[160,2560]{1,0:T(8,128)(2,1)S(1)} custom-call(s32[43]{0:T(128)S(1)} %concatenate.3.meta, bf16[640,640]{1,0:T(8,128)(2,1)} %bitcast.22.x_ref), custom_call_target="tpu_custom_call" | custom-call | flops 524288000 | bytes 1638400 | tf_op jit(solution)/shard_map/unpack/pallas_call | solution.py:101
  44.0 4.1 %collective-permute-start.7 = (bf16[160,2560]{1,0:T(8,128)(2,1)S(1)}, bf16[160,2560]{1,0:T(8,128)(2,1)S(1)}, u32[]{:S(2)}, u32[]{:S(2)}) collective-permute-start(bf16[160,2560]{1,0:T(8,128)(2,1)S(1)} %unpack.2.refs_0_), channel_id=1, source_target_pairs={{0,8},{1,9},{8,0},{9,1},{2,10},{3,11},{10,2},{11,3},{4,12},{5,13},... | collective-permute-start | bytes 2457608 | tf_op jit(solution)/shard_map/ppermute | solution.py:32
  48.1 1.5 right.2.refs_4_
  49.5 2.0 %collective-permute-start.11 = (bf16[320,640]{1,0:T(8,128)(2,1)S(1)}, bf16[320,640]{1,0:T(8,128)(2,1)S(1)}, u32[]{:S(2)}, u32[]{:S(2)}) collective-permute-start(bf16[320,640]{1,0:T(8,128)(2,1)S(1)} %right.2.refs_4_), channel_id=1, source_target_pairs={{0,4},{2,6},{4,0},{6,2},{1,5},{3,7},{5,1},{7,3},{8,12},{10,14},{12... | collective-permute-start | bytes 1228808 | tf_op jit(solution)/shard_map/ppermute | solution.py:28
  53.6 13.0 %collective-permute-done.7.refs_0_ = bf16[160,2560]{1,0:T(8,128)(2,1)S(1)} collective-permute-done((bf16[160,2560]{1,0:T(8,128)(2,1)S(1)}, bf16[160,2560]{1,0:T(8,128)(2,1)S(1)}, u32[]{:S(2)}, u32[]{:S(2)}) %collective-permute-start.7) | collective-permute-done | bytes 819232 | tf_op jit(solution)/shard_map/ppermute | solution.py:32
  66.6 4.9 %collective-permute-done.10.refs_6_ = bf16[320,640]{1,0:T(8,128)(2,1)S(1)} collective-permute-done((bf16[320,640]{1,0:T(8,128)(2,1)S(1)}, bf16[320,640]{1,0:T(8,128)(2,1)S(1)}, u32[]{:S(2)}, u32[]{:S(2)}) %collective-permute-start.10) | collective-permute-done | bytes 409632 | tf_op jit(solution)/shard_map/ppermute | solution.py:28
  71.4 2.3 %collective-permute-done.12.refs_1_ = bf16[160,2560]{1,0:T(8,128)(2,1)S(1)} collective-permute-done((bf16[160,2560]{1,0:T(8,128)(2,1)S(1)}, bf16[160,2560]{1,0:T(8,128)(2,1)S(1)}, u32[]{:S(2)}, u32[]{:S(2)}) %collective-permute-start.12) | collective-permute-done | bytes 819232 | tf_op jit(solution)/shard_map/ppermute | solution.py:32
  73.8 1.5 right.3.refs_4_
  75.2 1.7 %collective-permute-start.15 = (bf16[320,640]{1,0:T(8,128)(2,1)S(1)}, bf16[320,640]{1,0:T(8,128)(2,1)S(1)}, u32[]{:S(2)}, u32[]{:S(2)}) collective-permute-start(bf16[320,640]{1,0:T(8,128)(2,1)S(1)} %right.3.refs_4_), channel_id=1, source_target_pairs={{0,4},{2,6},{4,0},{6,2},{1,5},{3,7},{5,1},{7,3},{8,12},{10,14},{12... | collective-permute-start | bytes 1228808 | tf_op jit(solution)/shard_map/ppermute | solution.py:28
  76.9 1.3 collective-permute-start.14
  78.9 3.2 %left.2.refs_8_ = f32[640,640]{1,0:T(8,128)S(1)} custom-call(s32[43]{0:T(128)S(1)} %concatenate.3.meta, bf16[160,2560]{1,0:T(8,128)(2,1)} %bitcast.24.refs_0_, bf16[160,2560]{1,0:T(8,128)(2,1)S(1)} %copy-done.1, bf16[160,2560]{1,0:T(8,128)(2,1)} %collective-permute-done.5.refs_2_, bf16[160,2560]{1,0:T(8,128)(2,1)} %collective-permute-done.6.refs_3_, ...), custom_call_target="tpu_custom_call" | custom-call | flops 1048576000 | bytes 6553600 | tf_op jit(solution)/shard_map/left/pallas_call | solution.py:182
  82.2 7.0 %collective-permute-done.15.refs_7_ = bf16[320,640]{1,0:T(8,128)(2,1)S(1)} collective-permute-done((bf16[320,640]{1,0:T(8,128)(2,1)S(1)}, bf16[320,640]{1,0:T(8,128)(2,1)S(1)}, u32[]{:S(2)}, u32[]{:S(2)}) %collective-permute-start.15) | collective-permute-done | bytes 409632 | tf_op jit(solution)/shard_map/ppermute | solution.py:28
  89.2 7.7 %collective-permute-done.14.refs_6_ = bf16[320,640]{1,0:T(8,128)(2,1)S(1)} collective-permute-done((bf16[320,640]{1,0:T(8,128)(2,1)S(1)}, bf16[320,640]{1,0:T(8,128)(2,1)S(1)}, u32[]{:S(2)}, u32[]{:S(2)}) %collective-permute-start.14) | collective-permute-done | bytes 409632 | tf_op jit(solution)/shard_map/ppermute | solution.py:28
  97.1 3.2 %left.3 = (bf16[160,640]{1,0:T(8,128)(2,1)S(1)}, bf16[160,640]{1,0:T(8,128)(2,1)S(1)}, bf16[160,640]{1,0:T(8,128)(2,1)S(1)}, bf16[160,640]{1,0:T(8,128)(2,1)S(1)}) custom-call(s32[43]{0:T(128)S(1)} %concatenate.3.meta, bf16[160,2560]{1,0:T(8,128)(2,1)} %bitcast.24.refs_0_, bf16[160,2560]{1,0:T(8,128)(2,1)S(1)} %copy-done.1, ...), custom_call_target="tpu_custom_call" | custom-call | flops 1048576000 | bytes 6553600 | tf_op jit(solution)/shard_map/left/pallas_call | solution.py:182
  100.5 2.6 %collective-permute-start.17 = (bf16[160,640]{1,0:T(8,128)(2,1)S(1)}, bf16[160,640]{1,0:T(8,128)(2,1)S(1)}, u32[]{:S(2)}, u32[]{:S(2)}) collective-permute-start(bf16[160,640]{1,0:T(8,128)(2,1)S(1)} %get-tuple-element.27), channel_id=1, source_target_pairs={{0,8},{1,9},{8,0},{9,1},{2,10},{3,11},{10,2},{11,3},{4,12},{5,13},... | collective-permute-start | bytes 614408 | tf_op jit(solution)/shard_map/ppermute | solution.py:32
  103.8 6.1 %collective-permute-done.17.refs_2_ = bf16[160,640]{1,0:T(8,128)(2,1)S(1)} collective-permute-done((bf16[160,640]{1,0:T(8,128)(2,1)S(1)}, bf16[160,640]{1,0:T(8,128)(2,1)S(1)}, u32[]{:S(2)}, u32[]{:S(2)}) %collective-permute-start.17) | collective-permute-done | bytes 204832 | tf_op jit(solution)/shard_map/ppermute | solution.py:32
  109.9 3.4 %collective-permute-done.18.refs_3_ = bf16[160,640]{1,0:T(8,128)(2,1)S(1)} collective-permute-done((bf16[160,640]{1,0:T(8,128)(2,1)S(1)}, bf16[160,640]{1,0:T(8,128)(2,1)S(1)}, u32[]{:S(2)}, u32[]{:S(2)}) %collective-permute-start.18) | collective-permute-done | bytes 204832 | tf_op jit(solution)/shard_map/ppermute | solution.py:32
  113.4 1.7 %pack.3 = bf16[640,640]{1,0:T(8,128)(2,1)S(1)} custom-call(s32[43]{0:T(128)S(1)} %concatenate.3.meta, bf16[160,640]{1,0:T(8,128)(2,1)S(1)} %get-tuple-element.25.refs_0_, bf16[160,640]{1,0:T(8,128)(2,1)S(1)} %collective-permute-done.16.refs_1_, bf16[160,640]{1,0:T(8,128)(2,1)S(1)} %collective-permute-done.17.refs_2_, ...), custom_call_target="tpu_custom_call" | custom-call | flops 524288000 | bytes 1638400 | tf_op jit(solution)/shard_map/pack/pallas_call | solution.py:75
  115.1 32.2 %all_to_all.10 = bf16[16,40,640]{2,1,0:T(8,128)(2,1)S(1)} all-to-all(bf16[16,40,640]{2,1,0:T(8,128)(2,1)S(1)} %bitcast.31), channel_id=1, replica_groups=mesh['xl'=2,'z'=8,'xh'=2,'y'=4,'c'=2] {'xl','z'}, dimensions={0} | all-to-all | bytes 1638400 | tf_op jit(solution)/shard_map/all_to_all | solution.py:205
  147.3 2.4 %unpack.3 = bf16[160,2560]{1,0:T(8,128)(2,1)} custom-call(s32[43]{0:T(128)S(1)} %concatenate.3.meta, bf16[640,640]{1,0:T(8,128)(2,1)S(1)} %bitcast.32), custom_call_target="tpu_custom_call" | custom-call | flops 524288000 | bytes 1638400 | tf_op jit(solution)/shard_map/unpack/pallas_call | solution.py:101
  (38 shorter events, 6.3 us)
Async XLA Ops:
  0.0 20.8 %collective-permute-start.1 = (bf16[160,2560]{1,0:T(8,128)(2,1)}, bf16[160,2560]{1,0:T(8,128)(2,1)S(1)}, u32[]{:S(2)}, u32[]{:S(2)}) collective-permute-start(bf16[160,2560]{1,0:T(8,128)(2,1)} %bitcast.34), channel_id=1, source_target_pairs={{0,6},{2,0},{4,2},{6,4},{1,7},{3,1},{5,3},{7,5},{8,14},{10,8},{12,... | collective-permute-start | bytes 2457608 | tf_op jit(solution)/shard_map/ppermute | solution.py:28
  3.0 21.5 %collective-permute-start = (bf16[160,2560]{1,0:T(8,128)(2,1)}, bf16[160,2560]{1,0:T(8,128)(2,1)S(1)}, u32[]{:S(2)}, u32[]{:S(2)}) collective-permute-start(bf16[160,2560]{1,0:T(8,128)(2,1)} %bitcast.35), channel_id=1, source_target_pairs={{0,2},{2,4},{4,6},{6,0},{1,3},{3,5},{5,7},{7,1},{8,10},{10,12},{12... | collective-permute-start | bytes 2457608 | tf_op jit(solution)/shard_map/ppermute | solution.py:28
  3.8 1.1 copy-start.6
  7.6 28.0 %collective-permute-start.5 = (bf16[160,2560]{1,0:T(8,128)(2,1)}, bf16[160,2560]{1,0:T(8,128)(2,1)}, u32[]{:S(2)}, u32[]{:S(2)}) collective-permute-start(bf16[160,2560]{1,0:T(8,128)(2,1)} %bitcast.24.refs_0_), channel_id=1, source_target_pairs={{0,8},{1,9},{8,0},{9,1},{2,10},{3,11},{10,2},{11,3},{4,12},{5,13},... | collective-permute-start | bytes 2457608 | tf_op jit(solution)/shard_map/ppermute | solution.py:32
  10.6 31.0 %all-to-all-start = ((bf16[16,40,640]{2,1,0:T(8,128)(2,1)}), bf16[16,40,640]{2,1,0:T(8,128)(2,1)}, u32[]{:S(2)}, u32[]{:S(2)}) async-start(bf16[16,40,640]{2,1,0:T(8,128)(2,1)} %bitcast.21), calls=%async_computation | async-start | bytes 1638400 | tf_op jit(solution)/shard_map/all_to_all | solution.py:205
  20.8 14.8 %copy-start.2 = (bf16[160,2560]{1,0:T(8,128)(2,1)}, bf16[160,2560]{1,0:T(8,128)(2,1)S(1)}, u32[]{:S(2)}) copy-start(bf16[160,2560]{1,0:T(8,128)(2,1)S(1)} %collective-permute-done.1.refs_2_) | copy-start | bytes 2457604
  20.9 14.7 %collective-permute-start.3 = (bf16[80,2560]{1,0:T(8,128)(2,1)S(1)}, bf16[80,2560]{1,0:T(8,128)(2,1)S(1)}, u32[]{:S(2)}, u32[]{:S(2)}) collective-permute-start(bf16[80,2560]{1,0:T(8,128)(2,1)S(1)} %slice.9), channel_id=1, source_target_pairs={{0,6},{2,0},{4,2},{6,4},{1,7},{3,1},{5,3},{7,5},{8,14},{10,8},{12,... | collective-permute-start | bytes 1228808 | tf_op jit(solution)/shard_map/ppermute | solution.py:28
  24.5 11.1 %copy-start.4 = (bf16[160,2560]{1,0:T(8,128)(2,1)}, bf16[160,2560]{1,0:T(8,128)(2,1)S(1)}, u32[]{:S(2)}) copy-start(bf16[160,2560]{1,0:T(8,128)(2,1)S(1)} %collective-permute-done.refs_1_) | copy-start | bytes 2457604
  24.6 11.4 %collective-permute-start.2 = (bf16[80,2560]{1,0:T(8,128)(2,1)S(1)}, bf16[80,2560]{1,0:T(8,128)(2,1)S(1)}, u32[]{:S(2)}, u32[]{:S(2)}) collective-permute-start(bf16[80,2560]{1,0:T(8,128)(2,1)S(1)} %slice.8), channel_id=1, source_target_pairs={{0,2},{2,4},{4,6},{6,0},{1,3},{3,5},{5,7},{7,1},{8,10},{10,12},{12... | collective-permute-start | bytes 1228808 | tf_op jit(solution)/shard_map/ppermute | solution.py:28
  24.7 16.1 %collective-permute-start.4 = (bf16[160,2560]{1,0:T(8,128)(2,1)}, bf16[160,2560]{1,0:T(8,128)(2,1)S(1)}, u32[]{:S(2)}, u32[]{:S(2)}) collective-permute-start(bf16[160,2560]{1,0:T(8,128)(2,1)} %bitcast.24.refs_0_), channel_id=1, source_target_pairs={{0,1},{1,0},{8,9},{9,8},{2,3},{3,2},{10,11},{11,10},{4,5},{5,4},{1... | collective-permute-start | bytes 2457608 | tf_op jit(solution)/shard_map/ppermute | solution.py:32
  35.6 6.1 %collective-permute-start.6 = (bf16[160,2560]{1,0:T(8,128)(2,1)}, bf16[160,2560]{1,0:T(8,128)(2,1)}, u32[]{:S(2)}, u32[]{:S(2)}) collective-permute-start(bf16[160,2560]{1,0:T(8,128)(2,1)} %collective-permute-done.5.refs_2_), channel_id=1, source_target_pairs={{0,1},{1,0},{8,9},{9,8},{2,3},{3,2},{10,11},{11,10},{4,5},{5,4},{1... | collective-permute-start | bytes 2457608 | tf_op jit(solution)/shard_map/ppermute | solution.py:32
  36.0 1.1 copy-start.3
  37.2 1.1 copy-start.5
  38.3 1.1 copy-start.7
  40.8 0.9 copy-start
  43.8 4.3 %collective-permute-start.8 = (bf16[160,2560]{1,0:T(8,128)(2,1)S(1)}, bf16[160,2560]{1,0:T(8,128)(2,1)S(1)}, u32[]{:S(2)}, u32[]{:S(2)}) collective-permute-start(bf16[160,2560]{1,0:T(8,128)(2,1)S(1)} %unpack.2.refs_0_), channel_id=1, source_target_pairs={{0,1},{1,0},{8,9},{9,8},{2,3},{3,2},{10,11},{11,10},{4,5},{5,4},{1... | collective-permute-start | bytes 2457608 | tf_op jit(solution)/shard_map/ppermute | solution.py:32
  44.0 22.6 %collective-permute-start.7 = (bf16[160,2560]{1,0:T(8,128)(2,1)S(1)}, bf16[160,2560]{1,0:T(8,128)(2,1)S(1)}, u32[]{:S(2)}, u32[]{:S(2)}) collective-permute-start(bf16[160,2560]{1,0:T(8,128)(2,1)S(1)} %unpack.2.refs_0_), channel_id=1, source_target_pairs={{0,8},{1,9},{8,0},{9,1},{2,10},{3,11},{10,2},{11,3},{4,12},{5,13},... | collective-permute-start | bytes 2457608 | tf_op jit(solution)/shard_map/ppermute | solution.py:32
  49.5 29.4 %copy-start.1 = (bf16[160,2560]{1,0:T(8,128)(2,1)S(1)}, bf16[160,2560]{1,0:T(8,128)(2,1)}, u32[]{:S(2)}) copy-start(bf16[160,2560]{1,0:T(8,128)(2,1)} %copy-done) | copy-start | bytes 2457604
  49.5 17.0 %collective-permute-start.11 = (bf16[320,640]{1,0:T(8,128)(2,1)S(1)}, bf16[320,640]{1,0:T(8,128)(2,1)S(1)}, u32[]{:S(2)}, u32[]{:S(2)}) collective-permute-start(bf16[320,640]{1,0:T(8,128)(2,1)S(1)} %right.2.refs_4_), channel_id=1, source_target_pairs={{0,4},{2,6},{4,0},{6,2},{1,5},{3,7},{5,1},{7,3},{8,12},{10,14},{12... | collective-permute-start | bytes 1228808 | tf_op jit(solution)/shard_map/ppermute | solution.py:28
  51.5 19.9 %collective-permute-start.10 = (bf16[320,640]{1,0:T(8,128)(2,1)S(1)}, bf16[320,640]{1,0:T(8,128)(2,1)S(1)}, u32[]{:S(2)}, u32[]{:S(2)}) collective-permute-start(bf16[320,640]{1,0:T(8,128)(2,1)S(1)} %right.2.refs_4_), channel_id=1, source_target_pairs={{0,6},{2,0},{4,2},{6,4},{1,7},{3,1},{5,3},{7,5},{8,14},{10,8},{12,... | collective-permute-start | bytes 1228808 | tf_op jit(solution)/shard_map/ppermute | solution.py:28
  52.7 18.8 %collective-permute-start.9 = (bf16[320,640]{1,0:T(8,128)(2,1)S(1)}, bf16[320,640]{1,0:T(8,128)(2,1)S(1)}, u32[]{:S(2)}, u32[]{:S(2)}) collective-permute-start(bf16[320,640]{1,0:T(8,128)(2,1)S(1)} %right.2.refs_4_), channel_id=1, source_target_pairs={{0,2},{2,4},{4,6},{6,0},{1,3},{3,5},{5,7},{7,1},{8,10},{10,12},{12... | collective-permute-start | bytes 1228808 | tf_op jit(solution)/shard_map/ppermute | solution.py:28
  71.4 2.3 %collective-permute-start.12 = (bf16[160,2560]{1,0:T(8,128)(2,1)S(1)}, bf16[160,2560]{1,0:T(8,128)(2,1)S(1)}, u32[]{:S(2)}, u32[]{:S(2)}) collective-permute-start(bf16[160,2560]{1,0:T(8,128)(2,1)S(1)} %collective-permute-done.7.refs_0_), channel_id=1, source_target_pairs={{0,1},{1,0},{8,9},{9,8},{2,3},{3,2},{10,11},{11,10},{4,5},{5,4},{1... | collective-permute-start | bytes 2457608 | tf_op jit(solution)/shard_map/ppermute | solution.py:32
  75.2 13.9 %collective-permute-start.15 = (bf16[320,640]{1,0:T(8,128)(2,1)S(1)}, bf16[320,640]{1,0:T(8,128)(2,1)S(1)}, u32[]{:S(2)}, u32[]{:S(2)}) collective-permute-start(bf16[320,640]{1,0:T(8,128)(2,1)S(1)} %right.3.refs_4_), channel_id=1, source_target_pairs={{0,4},{2,6},{4,0},{6,2},{1,5},{3,7},{5,1},{7,3},{8,12},{10,14},{12... | collective-permute-start | bytes 1228808 | tf_op jit(solution)/shard_map/ppermute | solution.py:28
  76.9 20.0 %collective-permute-start.14 = (bf16[320,640]{1,0:T(8,128)(2,1)S(1)}, bf16[320,640]{1,0:T(8,128)(2,1)S(1)}, u32[]{:S(2)}, u32[]{:S(2)}) collective-permute-start(bf16[320,640]{1,0:T(8,128)(2,1)S(1)} %right.3.refs_4_), channel_id=1, source_target_pairs={{0,6},{2,0},{4,2},{6,4},{1,7},{3,1},{5,3},{7,5},{8,14},{10,8},{12,... | collective-permute-start | bytes 1228808 | tf_op jit(solution)/shard_map/ppermute | solution.py:28
  78.2 18.9 %collective-permute-start.13 = (bf16[320,640]{1,0:T(8,128)(2,1)S(1)}, bf16[320,640]{1,0:T(8,128)(2,1)S(1)}, u32[]{:S(2)}, u32[]{:S(2)}) collective-permute-start(bf16[320,640]{1,0:T(8,128)(2,1)S(1)} %right.3.refs_4_), channel_id=1, source_target_pairs={{0,2},{2,4},{4,6},{6,0},{1,3},{3,5},{5,7},{7,1},{8,10},{10,12},{12... | collective-permute-start | bytes 1228808 | tf_op jit(solution)/shard_map/ppermute | solution.py:28
  100.4 3.5 %collective-permute-start.16 = (bf16[160,640]{1,0:T(8,128)(2,1)S(1)}, bf16[160,640]{1,0:T(8,128)(2,1)S(1)}, u32[]{:S(2)}, u32[]{:S(2)}) collective-permute-start(bf16[160,640]{1,0:T(8,128)(2,1)S(1)} %get-tuple-element.26), channel_id=1, source_target_pairs={{0,1},{1,0},{8,9},{9,8},{2,3},{3,2},{10,11},{11,10},{4,5},{5,4},{1... | collective-permute-start | bytes 614408 | tf_op jit(solution)/shard_map/ppermute | solution.py:32
  100.5 9.5 %collective-permute-start.17 = (bf16[160,640]{1,0:T(8,128)(2,1)S(1)}, bf16[160,640]{1,0:T(8,128)(2,1)S(1)}, u32[]{:S(2)}, u32[]{:S(2)}) collective-permute-start(bf16[160,640]{1,0:T(8,128)(2,1)S(1)} %get-tuple-element.27), channel_id=1, source_target_pairs={{0,8},{1,9},{8,0},{9,1},{2,10},{3,11},{10,2},{11,3},{4,12},{5,13},... | collective-permute-start | bytes 614408 | tf_op jit(solution)/shard_map/ppermute | solution.py:32
  103.1 10.3 %collective-permute-start.18 = (bf16[160,640]{1,0:T(8,128)(2,1)S(1)}, bf16[160,640]{1,0:T(8,128)(2,1)S(1)}, u32[]{:S(2)}, u32[]{:S(2)}) collective-permute-start(bf16[160,640]{1,0:T(8,128)(2,1)S(1)} %get-tuple-element.28), channel_id=1, source_target_pairs={{0,9},{1,8},{8,1},{9,0},{2,11},{3,10},{10,3},{11,2},{4,13},{5,12},... | collective-permute-start | bytes 614408 | tf_op jit(solution)/shard_map/ppermute | solution.py:32
